TPU v7x, 32 devices: a whole 2x2x4 slice. The times are simulated.
32 devices in a mesh: groups: 2 (over y), seq: 4 (over z), head: 2 (over x), dp: 2 (over core).
Axes of the slice: x: 2, y: 2, z: 4, core: 2. Of those that a mesh axis runs over, the one named last changes fastest.
Arguments:
- inputs: bfloat16 [4, 2048, 3072], P(('groups', 'dp'), 'seq'), parts along dimension 0, may hold values from -6 to 6
- queries: bfloat16 [4, 2048, 4096], P(('groups', 'dp'), 'seq', 'head'), parts along dimension 0, may hold values from -6 to 6
- keys: bfloat16 [4, 2048, 4096], P(('groups', 'dp'), 'seq', 'head'), parts along dimension 0, may hold values from -6 to 6
- values: bfloat16 [4, 2048, 4096], P(('groups', 'dp'), 'seq', 'head'), parts along dimension 0, may hold values from -6 to 6
- log_decay: float32 [4, 32, 2048], P(('groups', 'dp'), 'head', 'seq'), parts along dimension 0, may hold values from -0.85 to 0, as said below
- list_lengths: int32 [4, 4], P(('groups', 'dp')), parts along dimension 0, may hold values from 1 to 1024, 2048 in all within a row
- grad_out: bfloat16 [4, 2048, 4096], P(('groups', 'dp'), 'seq', 'head'), parts along dimension 0, may hold values from -6 to 6
Outputs:
- grad_queries: bfloat16 [4, 2048, 4096], P(('groups', 'dp'), 'seq', 'head'), parts along dimension 0
- grad_values: bfloat16 [4, 2048, 4096], P(('groups', 'dp'), 'seq', 'head'), parts along dimension 0
- grad_w_key: float32 [6144, 4096], P(('groups', 'seq', 'dp'), 'head'), parts along dimension 0
There are 2 independent parts, one for each index of `groups`. A program takes and returns all parts, laid end to end along the dimension named above; each array names one. Nothing has to cross between parts.
Inputs may be any that keep to these rules, and one draw needn't show every extreme that they name: `list_lengths`: each row's 4 list lengths sum to 2048. `log_decay`: negative at every position and head.
All inputs are finite; a program needn't handle non-finite values.
Results may differ from a plain program's by a relative error of at most 0.02.
Values may be sent and summed in bfloat16 or wider, within the bound.
A program may use at most 192 MiB of HBM per device.

v0:
```python
import functools
import math

import jax
import jax.numpy as jnp
from jax import lax
from jax.experimental import pallas as pl
from jax.experimental.pallas import tpu as pltpu
from jax.sharding import PartitionSpec as P

EPS = 1e-06
MESH = pl.DeviceIdType.MESH
LANES = 128
F32 = jnp.float32
BF16 = jnp.bfloat16


def dot(a, b, ca, cb):
    return lax.dot_general(a, b, (((ca,), (cb,)), ((), ())), preferred_element_type=F32)


def greet(with_mate):
    barrier = pltpu.get_barrier_semaphore()
    me = lax.axis_index("seq")
    n = lax.axis_size("seq")

    @pl.when(me > 0)
    def _():
        pl.semaphore_signal(barrier, inc=1, device_id={"seq": me - 1}, device_id_type=MESH)

    @pl.when(me < n - 1)
    def _():
        pl.semaphore_signal(barrier, inc=1, device_id={"seq": me + 1}, device_id_type=MESH)

    peers = (me > 0).astype(jnp.int32) + (me < n - 1).astype(jnp.int32)
    if with_mate:
        mate = 1 - lax.axis_index("dp")
        pl.semaphore_signal(barrier, inc=1, device_id={"dp": mate}, device_id_type=MESH)
        peers = peers + 1
    pl.semaphore_wait(barrier, peers)


def attention_kernel(
    heads, ll_ref, ld_ref, q_ref, k_ref, v_ref, g_ref, gq_ref, gv_ref, gk_ref,
    cum_ref, colb_ref, mask_ref, min_ref, mout_ref, upd_ref, att_ref, sc_ref, ga_ref,
    bs_ref, ki_ref, vi_ref, fsend, frecv, bsend, brecv, fss, frs, bss, brs,
):
    n = lax.axis_size("seq")
    me = lax.axis_index("seq")
    B = q_ref.shape[0]
    group = math.gcd(heads, 4)
    groups = heads // group
    tile = math.gcd(B, 256)
    tiles = B // tile
    first = me * B

    greet(False)

    lengths = [ll_ref[0, i] for i in range(ll_ref.shape[1])]
    starts = [jnp.int32(0)]
    for length in lengths[:-1]:
        starts.append(starts[-1] + length)

    def seg_of(pos):
        total = (starts[0] <= pos).astype(jnp.int32)
        for s in starts[1:]:
            total = total + (s <= pos).astype(jnp.int32)
        return total

    before = seg_of(first - 1)
    end = seg_of(first + B - 1)
    seg_col = seg_of(first + lax.broadcasted_iota(jnp.int32, (B, LANES), 0))
    min_ref[...] = jnp.where(seg_col == before, 1.0, 0.0).astype(F32)
    mout_ref[...] = jnp.where(seg_col == end, 1.0, 0.0).astype(F32)
    open_all = jnp.where(jnp.full((1, LANES), end) == before, 1.0, 0.0).astype(F32)
    t_pos = lax.broadcasted_iota(jnp.int32, (B, B), 0)
    u_pos = lax.broadcasted_iota(jnp.int32, (B, B), 1)
    same = (t_pos >= u_pos) & (seg_of(first + t_pos) == seg_of(first + u_pos))
    mask_ref[...] = jnp.where(same, 0.0, -1e30).astype(F32)
    tri = jnp.where(t_pos <= u_pos, 1.0, 0.0).astype(F32)
    cum_ref[...] = lax.dot_general(
        ld_ref[...], tri, (((1,), (0,)), ((), ())),
        preferred_element_type=F32, precision=lax.Precision.HIGHEST,
    )

    def lanes(h):
        return pl.ds(pl.multiple_of(h * LANES, LANES), LANES)

    def weight_of(h):
        cb = colb_ref[h]
        return jnp.exp(cb[B - 1 : B, :] - cb) * mout_ref[...]

    def gamma_of(h):
        return jnp.exp(colb_ref[h]) * min_ref[...]

    def passing_of(h):
        return jnp.exp(colb_ref[h, B - 1 : B, :]) * open_all

    def decay_of(h, i):
        ts, cols = slice(i * tile, (i + 1) * tile), (i + 1) * tile
        cb = colb_ref[h, ts, :]
        wide = jnp.concatenate([cb] * (cols // LANES), axis=1)
        row = cum_ref[pl.ds(h, 1), :cols]
        return jnp.exp((wide - row) + mask_ref[ts, :cols])

    def hop(src, dst, ss, rs, g, to):
        span = pl.ds(g * group, group)
        return pltpu.make_async_remote_copy(
            src_ref=src.at[span], dst_ref=dst.at[span], send_sem=ss.at[g], recv_sem=rs.at[g],
            device_id={"seq": to}, device_id_type=MESH,
        )

    def forward(g):
        return hop(fsend, frecv, fss, frs, g, me + 1)

    def backward(g):
        return hop(bsend, brecv, bss, brs, g, me - 1)

    def each_head(g, body):
        def step(i, c):
            body(g * group + i, i)
            return c
        lax.fori_loop(0, group, step, 0)

    def update_group(g, c):
        def one(h, i):
            colb_ref[h] = jnp.transpose(jnp.broadcast_to(cum_ref[pl.ds(h, 1), :], (LANES, B)))
            wk = (k_ref[:, lanes(h)].astype(F32) * weight_of(h)).astype(BF16)
            upd = dot(wk, v_ref[:, lanes(h)], 0, 0)
            upd_ref[h] = upd

            @pl.when(me == 0)
            def _():
                fsend[h] = upd.astype(BF16)
                frecv[h] = jnp.zeros((LANES, LANES), BF16)

            @pl.when(me == n - 1)
            def _():
                brecv[h] = jnp.zeros((LANES, LANES), BF16)

        each_head(g, one)

        @pl.when((me == 0) & (n > 1))
        def _():
            forward(g).start()
        return c

    lax.fori_loop(0, groups, update_group, 0)

    def intra_group(g, c):
        def one(h, i):
            for b in range(tiles):
                ts, cols = slice(b * tile, (b + 1) * tile), (b + 1) * tile
                s = dot(q_ref[ts, lanes(h)], k_ref[:cols, lanes(h)], 1, 1)
                s_bf = (s * decay_of(h, b)).astype(BF16)
                sc_ref[h, ts, :cols] = s_bf
                att_ref[h, ts, :] = dot(s_bf, v_ref[:cols, lanes(h)], 1, 0)

        each_head(g, one)

        @pl.when(me > 0)
        def _():
            forward(g).wait_recv()

        @pl.when((me > 0) & (me < n - 1))
        def _():
            def send(h, i):
                fsend[h] = (passing_of(h) * frecv[h].astype(F32) + upd_ref[h]).astype(BF16)
            each_head(g, send)
            forward(g).start()
        return c

    lax.fori_loop(0, groups, intra_group, 0)

    def attend_group(g, c):
        def one(h, i):
            gamma = gamma_of(h)
            q = q_ref[:, lanes(h)]
            att = gamma * dot(q, frecv[h], 1, 0) + att_ref[h]
            inv = lax.rsqrt(jnp.mean(att * att, axis=-1, keepdims=True) + EPS)
            normed = att * inv
            wide = g_ref[:, lanes(h)].astype(F32)
            ga = (inv * (wide - normed * jnp.mean(wide * normed, axis=-1, keepdims=True))).astype(BF16)
            ga_ref[h] = ga
            gated = (q.astype(F32) * gamma).astype(BF16)
            bs = dot(gated, ga, 0, 0)
            bs_ref[h] = bs

            @pl.when(me == n - 1)
            def _():
                bsend[h] = bs.astype(BF16)

        each_head(g, one)

        @pl.when((me == n - 1) & (n > 1))
        def _():
            backward(g).start()
        return c

    lax.fori_loop(0, groups, attend_group, 0)

    def grads_group(g, c):
        def one(h, i):
            gamma = gamma_of(h)
            kis, vis = [None] * tiles, [None] * tiles
            for b in range(tiles):
                ts, cols = slice(b * tile, (b + 1) * tile), (b + 1) * tile
                ga = ga_ref[h, ts, :]
                gs = (dot(ga, v_ref[:cols, lanes(h)], 1, 1) * decay_of(h, b)).astype(BF16)
                gq = gamma[ts] * dot(ga, frecv[h], 1, 1) + dot(gs, k_ref[:cols, lanes(h)], 1, 0)
                gq_ref[ts, lanes(h)] = gq.astype(BF16)
                ki = dot(gs, q_ref[ts, lanes(h)], 0, 0)
                vi = dot(sc_ref[h, ts, :cols], ga, 0, 0)
                for j in range(b + 1):
                    js = slice(j * tile, (j + 1) * tile)
                    kis[j] = ki[js] if kis[j] is None else kis[j] + ki[js]
                    vis[j] = vi[js] if vis[j] is None else vis[j] + vi[js]
            for j in range(tiles):
                ki_ref[i, j * tile : (j + 1) * tile, :] = kis[j]
                vi_ref[i, j * tile : (j + 1) * tile, :] = vis[j]

        each_head(g, one)

        @pl.when(me < n - 1)
        def _():
            backward(g).wait_recv()

        @pl.when((me > 0) & (me < n - 1))
        def _():
            def send(h, i):
                bsend[h] = (passing_of(h) * brecv[h].astype(F32) + bs_ref[h]).astype(BF16)
            each_head(g, send)
            backward(g).start()

        def finish(h, i):
            w = weight_of(h)
            later = brecv[h]
            gk_ref[:, lanes(h)] = (ki_ref[i] + w * dot(v_ref[:, lanes(h)], later, 1, 1)).astype(BF16)
            gv_ref[:, lanes(h)] = (vi_ref[i] + w * dot(k_ref[:, lanes(h)], later, 1, 0)).astype(BF16)

        each_head(g, finish)
        return c

    lax.fori_loop(0, groups, grads_group, 0)

    def drain(g, c):
        @pl.when(me < n - 1)
        def _():
            forward(g).wait_send()

        @pl.when(me > 0)
        def _():
            backward(g).wait_send()
        return c

    lax.fori_loop(0, groups, drain, 0)


def attention(lengths, log_decay, q, k, v, g):
    heads, B = log_decay.shape
    F = q.shape[-1]
    group = math.gcd(heads, 4)
    groups = heads // group
    vmem = pl.BlockSpec(memory_space=pltpu.VMEM)
    state = (heads, LANES, LANES)
    out = jax.ShapeDtypeStruct((B, F), BF16)
    return pl.pallas_call(
        functools.partial(attention_kernel, heads),
        out_shape=(out, out, out),
        in_specs=[pl.BlockSpec(memory_space=pltpu.SMEM)] + [vmem] * 5,
        out_specs=(vmem, vmem, vmem),
        scratch_shapes=[
            pltpu.VMEM((heads, B), F32),
            pltpu.VMEM((heads, B, LANES), F32),
            pltpu.VMEM((B, B), F32),
            pltpu.VMEM((B, LANES), F32),
            pltpu.VMEM((B, LANES), F32),
            pltpu.VMEM(state, F32),
            pltpu.VMEM((heads, B, LANES), F32),
            pltpu.VMEM((heads, B, B), BF16),
            pltpu.VMEM((heads, B, LANES), BF16),
            pltpu.VMEM(state, F32),
            pltpu.VMEM((group, B, LANES), F32),
            pltpu.VMEM((group, B, LANES), F32),
            pltpu.VMEM(state, BF16),
            pltpu.VMEM(state, BF16),
            pltpu.VMEM(state, BF16),
            pltpu.VMEM(state, BF16),
        ]
        + [pltpu.SemaphoreType.DMA((groups,))] * 4,
        compiler_params=pltpu.CompilerParams(
            collective_id=0, has_side_effects=True, vmem_limit_bytes=56 * 1024 * 1024
        ),
        name="attention",
    )(lengths, log_decay, q, k, v, g)


def weight_kernel(subs, xt_ref, gk_ref, out_ref, xm_ref, gm_ref, st_ref, msend, mrecv, ss, rs):
    n = lax.axis_size("seq")
    me = lax.axis_index("seq")
    dp = lax.axis_index("dp")
    mate = 1 - dp
    F = gk_ref.shape[1]
    width = F // subs

    greet(True)

    def to_mate(src, dst, i):
        return pltpu.make_async_remote_copy(
            src_ref=src, dst_ref=dst, send_sem=msend.at[i], recv_sem=mrecv.at[i],
            device_id={"dp": mate}, device_id_type=MESH,
        )

    copies = [to_mate(gk_ref, gm_ref, 0), to_mate(xt_ref.at[mate], xm_ref, 1)]
    for c in copies:
        c.start()
    for c in copies:
        c.wait()

    def partial(z, sub):
        span = pl.ds(pl.multiple_of(sub * width, LANES), width)
        own = dot(xt_ref[dp, z], gk_ref[:, span], 1, 0)
        return own + dot(xm_ref[z], gm_ref[:, span], 1, 0)

    def copy(d, z, sub):
        return pltpu.make_async_remote_copy(
            src_ref=st_ref.at[d, z, sub], dst_ref=st_ref.at[d, z, sub],
            send_sem=ss.at[d, z, sub], recv_sem=rs.at[d, z, sub],
            device_id={"seq": me + 1 - 2 * d}, device_id_type=MESH,
        )

    flip = (me >= n // 2).astype(jnp.int32)

    def step(i, c):
        s = i // (2 * subs)
        sub = (i // 2) % subs
        d = (i + flip) % 2
        z = s + (1 - d) * (n - 1 - 2 * s)
        active = (1 - 2 * d) * (z - me) > 0
        inner = (1 - d) * me + d * (n - 1 - me) > 0

        @pl.when(active)
        def _():
            total = partial(z, sub)

            @pl.when(inner)
            def _():
                copy(d, z, sub).wait_recv()
                st_ref[d, z, sub] = (total + st_ref[d, z, sub].astype(F32)).astype(BF16)

            @pl.when(jnp.logical_not(inner))
            def _():
                st_ref[d, z, sub] = total.astype(BF16)

            copy(d, z, sub).start()
        return c

    lax.fori_loop(0, (n - 1) * subs * 2, step, 0)

    for sub in range(subs):
        span = slice(sub * width, (sub + 1) * width)
        out_ref[:, span] = partial(me, sub)
    for sub in range(subs):
        span = slice(sub * width, (sub + 1) * width)

        @pl.when(me > 0)
        def _():
            copy(0, me, sub).wait_recv()
            out_ref[:, span] += st_ref[0, me, sub].astype(F32)

        @pl.when(me < n - 1)
        def _():
            copy(1, me, sub).wait_recv()
            out_ref[:, span] += st_ref[1, me, sub].astype(F32)

    def drain(i, c):
        s = i // (2 * subs)
        sub = (i // 2) % subs
        d = i % 2
        z = s + (1 - d) * (n - 1 - 2 * s)

        @pl.when((1 - 2 * d) * (z - me) > 0)
        def _():
            copy(d, z, sub).wait_send()
        return c

    lax.fori_loop(0, (n - 1) * subs * 2, drain, 0)


def weight_gradient(inputs, gk):
    n = lax.axis_size("seq")
    mates = lax.axis_size("dp")
    B, D = inputs.shape
    F = gk.shape[1]
    rows = D // (n * mates)
    subs = 4
    xt = inputs.T.reshape(n, mates, rows, B).transpose(1, 0, 2, 3)
    vmem = pl.BlockSpec(memory_space=pltpu.VMEM)
    return pl.pallas_call(
        functools.partial(weight_kernel, subs),
        out_shape=jax.ShapeDtypeStruct((rows, F), F32),
        in_specs=[vmem, vmem],
        out_specs=vmem,
        scratch_shapes=[
            pltpu.VMEM((n, rows, B), BF16),
            pltpu.VMEM((B, F), BF16),
            pltpu.VMEM((2, n, subs, rows, F // subs), BF16),
            pltpu.SemaphoreType.DMA((2,)),
            pltpu.SemaphoreType.DMA((2,)),
            pltpu.SemaphoreType.DMA((2, n, subs)),
            pltpu.SemaphoreType.DMA((2, n, subs)),
        ],
        compiler_params=pltpu.CompilerParams(
            collective_id=1, has_side_effects=True, vmem_limit_bytes=56 * 1024 * 1024
        ),
        name="weight_gradient",
    )(xt, gk)


def body(inputs, queries, keys, values, log_decay, list_lengths, grad_out):
    gq, gv, gk = attention(
        list_lengths, log_decay[0], queries[0], keys[0], values[0], grad_out[0]
    )
    return gq[None], gv[None], weight_gradient(inputs[0], gk)


def solution(mesh):
    rows = ("groups", "dp")
    wide = P(rows, "seq", "head")
    return jax.shard_map(
        body,
        mesh=mesh,
        in_specs=(
            P(rows, "seq", None), wide, wide, wide, P(rows, "head", "seq"), P(rows, None), wide,
        ),
        out_specs=(wide, wide, P(("groups", "seq", "dp"), "head")),
        check_vma=False,
    )
```

profile of v0, /device:TPU:9, one launch (start us, length us, event | category | flops | bytes accessed | tf_op | source)
XLA Modules:
  0.0 191.2 jit_solution(17457049719998513190)
XLA Ops:
  0.6 3.2 %copy.10 = bf16[1,512,3072]{1,2,0:T(8,128)(2,1)S(1)} copy(bf16[1,512,3072]{2,1,0:T(8,128)(2,1)} %param.7) | data formatting | bytes 6291456 | tf_op args[0]
  3.8 1.9 copy.13
  5.7 58.8 %attention.1 = (bf16[512,2048]{1,0:T(8,128)(2,1)}, bf16[512,2048]{1,0:T(8,128)(2,1)}, bf16[512,2048]{1,0:T(8,128)(2,1)}) custom-call(s32[1,4]{1,0:T(1,128)} %ll_ref.1, f32[16,512]{1,0:T(8,128)} %bitcast.23, bf16[512,2048]{1,0:T(8,128)(2,1)} %bitcast.19, bf16[512,2048]{1,0:T(8,128)(2,1)} %bitcast.20, bf16[512,2048]{1,0:T(8,128)(2,1)} %bitcast.21, ...), custom_call_target="tpu_custom_call" | custom-call | tf_op jit(solution)/shard_map/attention/pallas_call | solution.py:267
  64.5 0.0 copy-start.2
  64.5 119.9 %weight_gradient.1 = f32[384,2048]{1,0:T(8,128)} custom-call(bf16[2,4,384,512]{3,2,1,0:T(8,128)(2,1)} %bitcast.16, bf16[512,2048]{1,0:T(8,128)(2,1)} %get-tuple-element.8.gk_ref), custom_call_target="tpu_custom_call" | custom-call | tf_op jit(solution)/shard_map/weight_gradient/pallas_call | solution.py:399
  184.5 0.0 copy-done.2
  184.5 0.0 copy-start.1
  184.5 1.3 copy.17
  185.8 1.0 copy-done.1
  186.8 0.0 copy-start
  186.9 1.3 copy.18
  188.2 1.3 copy-done
  189.5 1.7 copy.19
Async XLA Ops:
  64.5 120.0 %copy-start.2 = (bf16[512,2048]{1,0:T(8,128)(2,1)S(1)}, bf16[512,2048]{1,0:T(8,128)(2,1)}, u32[]{:S(2)}) copy-start(bf16[512,2048]{1,0:T(8,128)(2,1)} %get-tuple-element.6) | copy-start | bytes 6291460
  184.5 2.3 %copy-start.1 = (bf16[512,2048]{1,0:T(8,128)(2,1)S(1)}, bf16[512,2048]{1,0:T(8,128)(2,1)}, u32[]{:S(2)}) copy-start(bf16[512,2048]{1,0:T(8,128)(2,1)} %get-tuple-element.7) | copy-start | bytes 6291460
  186.8 2.6 %copy-start = (f32[384,2048]{1,0:T(8,128)S(1)}, f32[384,2048]{1,0:T(8,128)}, u32[]{:S(2)}) copy-start(f32[384,2048]{1,0:T(8,128)} %weight_gradient.1) | copy-start | bytes 9437188
where the time goes:
time: 192 us; the launch traced here: 191 us
  Pallas kernels  179 us (93%)
  local copies, waits for them, and re-layouts  11.7 us (6%)
    pallas_call x1, Pallas kernels, weight_gradient(): pl.pallas_call(functools.partial(weight_kernel, subs), out_shape=jax.Shap...  120 us
    pallas_call x1, Pallas kernels, attention(): pl.pallas_call(functools.partial(attention_kernel, heads), out_shape=(out...  58.8 us
    unnamed x10, local copies, waits for them, and re-layouts  9.84 us

commit v1 on v0

v1 whole, which is shorter than its diff:
```python
import functools
import math

import jax
import jax.numpy as jnp
from jax import lax
from jax.experimental import pallas as pl
from jax.experimental.pallas import tpu as pltpu
from jax.sharding import PartitionSpec as P

EPS = 1e-06
MESH = pl.DeviceIdType.MESH
LANES = 128
F32 = jnp.float32
BF16 = jnp.bfloat16


def dot(a, b, ca, cb):
    return lax.dot_general(a, b, (((ca,), (cb,)), ((), ())), preferred_element_type=F32)


def greet(with_mate):
    barrier = pltpu.get_barrier_semaphore()
    me = lax.axis_index("seq")
    n = lax.axis_size("seq")

    @pl.when(me > 0)
    def _():
        pl.semaphore_signal(barrier, inc=1, device_id={"seq": me - 1}, device_id_type=MESH)

    @pl.when(me < n - 1)
    def _():
        pl.semaphore_signal(barrier, inc=1, device_id={"seq": me + 1}, device_id_type=MESH)

    peers = (me > 0).astype(jnp.int32) + (me < n - 1).astype(jnp.int32)
    if with_mate:
        mate = 1 - lax.axis_index("dp")
        pl.semaphore_signal(barrier, inc=1, device_id={"dp": mate}, device_id_type=MESH)
        peers = peers + 1
    pl.semaphore_wait(barrier, peers)


def layer_kernel(
    heads, ll_ref, ld_ref, x_hbm, q_hbm, k_hbm, v_hbm, g_hbm, gq_hbm, gv_hbm, gw_hbm,
    q_ref, k_ref, v_ref, g_ref, x_ref, xt_ref, xm_ref, gm_ref, st_ref, out_ref,
    cum_ref, colb_ref, mask_ref, min_ref, mout_ref, upd_ref, att_ref, sc_ref, ga_ref,
    bs_ref, ki_ref, vi_ref, fsend, frecv, bsend, brecv, fss, frs, bss, brs,
    load_sem, x_sem, store_sem, xss, xrs, gss, grs, ss, rs,
):
    n = lax.axis_size("seq")
    me = lax.axis_index("seq")
    B = q_ref.shape[0]
    group = math.gcd(heads, 4)
    groups = heads // group
    tile = math.gcd(B, 256)
    tiles = B // tile
    first = me * B
    dp = lax.axis_index("dp")
    mate = 1 - dp
    D = x_ref.shape[1]
    rows = D // (2 * n)
    width = group * LANES

    def columns(g):
        return pl.ds(pl.multiple_of(g * width, LANES), width)

    def load(a, g):
        src = (k_hbm, v_hbm, q_hbm, g_hbm)[a]
        dst = (k_ref, v_ref, q_ref, g_ref)[a]
        return pltpu.make_async_copy(
            src.at[:, columns(g)], dst.at[:, columns(g)], load_sem.at[a, g]
        )

    def store(a, g):
        src, dst = ((q_ref, gq_hbm), (g_ref, gv_hbm), (out_ref, gw_hbm))[a]
        return pltpu.make_async_copy(
            src.at[:, columns(g)], dst.at[:, columns(g)], store_sem.at[a, g]
        )

    def each_group(body):
        def step(g, c):
            body(g)
            return c
        lax.fori_loop(0, groups, step, 0)

    def load_kv(g):
        load(0, g).start()
        load(1, g).start()

    each_group(load_kv)
    load_x = pltpu.make_async_copy(x_hbm, x_ref, x_sem)
    load_x.start()
    each_group(lambda g: load(2, g).start())
    each_group(lambda g: load(3, g).start())

    greet(True)

    lengths = [ll_ref[0, i] for i in range(ll_ref.shape[1])]
    starts = [jnp.int32(0)]
    for length in lengths[:-1]:
        starts.append(starts[-1] + length)

    def seg_of(pos):
        total = (starts[0] <= pos).astype(jnp.int32)
        for s in starts[1:]:
            total = total + (s <= pos).astype(jnp.int32)
        return total

    before = seg_of(first - 1)
    end = seg_of(first + B - 1)
    seg_col = seg_of(first + lax.broadcasted_iota(jnp.int32, (B, LANES), 0))
    min_ref[...] = jnp.where(seg_col == before, 1.0, 0.0).astype(F32)
    mout_ref[...] = jnp.where(seg_col == end, 1.0, 0.0).astype(F32)
    open_all = jnp.where(jnp.full((1, LANES), end) == before, 1.0, 0.0).astype(F32)
    t_pos = lax.broadcasted_iota(jnp.int32, (B, B), 0)
    u_pos = lax.broadcasted_iota(jnp.int32, (B, B), 1)
    same = (t_pos >= u_pos) & (seg_of(first + t_pos) == seg_of(first + u_pos))
    mask_ref[...] = jnp.where(same, 0.0, -1e30).astype(F32)
    tri = jnp.where(t_pos <= u_pos, 1.0, 0.0).astype(F32)
    cum_ref[...] = lax.dot_general(
        ld_ref[...], tri, (((1,), (0,)), ((), ())),
        preferred_element_type=F32, precision=lax.Precision.HIGHEST,
    )

    def lanes(h):
        return pl.ds(pl.multiple_of(h * LANES, LANES), LANES)

    def weight_of(h):
        cb = colb_ref[h]
        return jnp.exp(cb[B - 1 : B, :] - cb) * mout_ref[...]

    def gamma_of(h):
        return jnp.exp(colb_ref[h]) * min_ref[...]

    def passing_of(h):
        return jnp.exp(colb_ref[h, B - 1 : B, :]) * open_all

    def decay_of(h, i):
        ts, cols = slice(i * tile, (i + 1) * tile), (i + 1) * tile
        cb = colb_ref[h, ts, :]
        wide = jnp.concatenate([cb] * (cols // LANES), axis=1)
        row = cum_ref[pl.ds(h, 1), :cols]
        return jnp.exp((wide - row) + mask_ref[ts, :cols])

    def hop(src, dst, ss, rs, g, to):
        span = pl.ds(g * group, group)
        return pltpu.make_async_remote_copy(
            src_ref=src.at[span], dst_ref=dst.at[span], send_sem=ss.at[g], recv_sem=rs.at[g],
            device_id={"seq": to}, device_id_type=MESH,
        )

    def forward(g):
        return hop(fsend, frecv, fss, frs, g, me + 1)

    def backward(g):
        return hop(bsend, brecv, bss, brs, g, me - 1)

    def each_head(g, body):
        def step(i, c):
            body(g * group + i, i)
            return c
        lax.fori_loop(0, group, step, 0)

    def update_group(g, c):
        load(0, g).wait()
        load(1, g).wait()

        def one(h, i):
            colb_ref[h] = jnp.transpose(jnp.broadcast_to(cum_ref[pl.ds(h, 1), :], (LANES, B)))
            wk = (k_ref[:, lanes(h)].astype(F32) * weight_of(h)).astype(BF16)
            upd = dot(wk, v_ref[:, lanes(h)], 0, 0)
            upd_ref[h] = upd

            @pl.when(me == 0)
            def _():
                fsend[h] = upd.astype(BF16)
                frecv[h] = jnp.zeros((LANES, LANES), BF16)

            @pl.when(me == n - 1)
            def _():
                brecv[h] = jnp.zeros((LANES, LANES), BF16)

        each_head(g, one)

        @pl.when((me == 0) & (n > 1))
        def _():
            forward(g).start()
        return c

    lax.fori_loop(0, groups, update_group, 0)

    load_x.wait()

    def turn(i, c):
        span = pl.ds(pl.multiple_of(i * LANES, LANES), LANES)
        xt_ref[span, :] = jnp.transpose(x_ref[:, span])
        return c

    lax.fori_loop(0, D // LANES, turn, 0)

    def share(z, owner):
        return pl.ds(pl.multiple_of((z * 2 + owner) * rows, math.gcd(rows, LANES)), rows)

    def x_copy(z):
        return pltpu.make_async_remote_copy(
            src_ref=xt_ref.at[share(z, mate)], dst_ref=xm_ref.at[z],
            send_sem=xss.at[z], recv_sem=xrs.at[z],
            device_id={"dp": mate}, device_id_type=MESH,
        )

    def send_x(z, c):
        x_copy(z).start()
        return c

    lax.fori_loop(0, n, send_x, 0)

    def intra_group(g, c):
        load(2, g).wait()

        def one(h, i):
            for b in range(tiles):
                ts, cols = slice(b * tile, (b + 1) * tile), (b + 1) * tile
                s = dot(q_ref[ts, lanes(h)], k_ref[:cols, lanes(h)], 1, 1)
                s_bf = (s * decay_of(h, b)).astype(BF16)
                sc_ref[h, ts, :cols] = s_bf
                att_ref[h, ts, :] = dot(s_bf, v_ref[:cols, lanes(h)], 1, 0)

        each_head(g, one)

        @pl.when(me > 0)
        def _():
            forward(g).wait_recv()

        @pl.when((me > 0) & (me < n - 1))
        def _():
            def send(h, i):
                fsend[h] = (passing_of(h) * frecv[h].astype(F32) + upd_ref[h]).astype(BF16)
            each_head(g, send)
            forward(g).start()
        return c

    lax.fori_loop(0, groups, intra_group, 0)

    def attend_group(g, c):
        load(3, g).wait()

        def one(h, i):
            gamma = gamma_of(h)
            q = q_ref[:, lanes(h)]
            att = gamma * dot(q, frecv[h], 1, 0) + att_ref[h]
            inv = lax.rsqrt(jnp.mean(att * att, axis=-1, keepdims=True) + EPS)
            normed = att * inv
            wide = g_ref[:, lanes(h)].astype(F32)
            ga = (inv * (wide - normed * jnp.mean(wide * normed, axis=-1, keepdims=True))).astype(BF16)
            ga_ref[h] = ga
            gated = (q.astype(F32) * gamma).astype(BF16)
            bs = dot(gated, ga, 0, 0)
            bs_ref[h] = bs

            @pl.when(me == n - 1)
            def _():
                bsend[h] = bs.astype(BF16)

        each_head(g, one)

        @pl.when((me == n - 1) & (n > 1))
        def _():
            backward(g).start()
        return c

    lax.fori_loop(0, groups, attend_group, 0)

    def gk_copy(g):
        return pltpu.make_async_remote_copy(
            src_ref=k_ref.at[:, columns(g)], dst_ref=gm_ref.at[:, columns(g)],
            send_sem=gss.at[g], recv_sem=grs.at[g],
            device_id={"dp": mate}, device_id_type=MESH,
        )

    def relay_back(g):
        @pl.when(me < n - 1)
        def _():
            backward(g).wait_recv()

        @pl.when((me > 0) & (me < n - 1))
        def _():
            def send(h, i):
                bsend[h] = (passing_of(h) * brecv[h].astype(F32) + bs_ref[h]).astype(BF16)
            each_head(g, send)
            backward(g).start()

    def partial(z, g):
        own = dot(xt_ref[share(z, dp), :], k_ref[:, columns(g)], 1, 0)
        return own + dot(xm_ref[z], gm_ref[:, columns(g)], 1, 0)

    def term(d, z, g):
        to = me + 1 - 2 * d
        slot = jnp.where((d == 1) & (to == z), n, z)
        return pltpu.make_async_remote_copy(
            src_ref=st_ref.at[z, g], dst_ref=st_ref.at[slot, g],
            send_sem=ss.at[z, g], recv_sem=rs.at[slot, g],
            device_id={"seq": to}, device_id_type=MESH,
        )

    def arrived(slot, g):
        pltpu.make_async_remote_copy(
            src_ref=st_ref.at[slot, g], dst_ref=st_ref.at[slot, g],
            send_sem=ss.at[0, g], recv_sem=rs.at[slot, g],
            device_id={"dp": mate}, device_id_type=MESH,
        ).wait_recv()

    flip = (me >= n // 2).astype(jnp.int32)

    def route(i):
        s = i // 2
        d = (i + flip) % 2
        z = s + (1 - d) * (n - 1 - 2 * s)
        return d, z, (1 - 2 * d) * (z - me) > 0

    def scatter(g):
        def step(i, c):
            d, z, active = route(i)
            inner = (1 - d) * me + d * (n - 1 - me) > 0

            @pl.when(active)
            def _():
                total = partial(z, g)

                @pl.when(inner)
                def _():
                    arrived(z, g)
                    st_ref[z, g] = (total + st_ref[z, g].astype(F32)).astype(BF16)

                @pl.when(jnp.logical_not(inner))
                def _():
                    st_ref[z, g] = total.astype(BF16)

                term(d, z, g).start()
            return c

        lax.fori_loop(0, (n - 1) * 2, step, 0)
        out_ref[:, columns(g)] = partial(me, g)

    def grads_group(g, c):
        def one(h, i):
            gamma = gamma_of(h)
            kis, vis = [None] * tiles, [None] * tiles
            for b in range(tiles):
                ts, cols = slice(b * tile, (b + 1) * tile), (b + 1) * tile
                ga = ga_ref[h, ts, :]
                q = q_ref[ts, lanes(h)]
                gs = (dot(ga, v_ref[:cols, lanes(h)], 1, 1) * decay_of(h, b)).astype(BF16)
                gq = gamma[ts] * dot(ga, frecv[h], 1, 1) + dot(gs, k_ref[:cols, lanes(h)], 1, 0)
                ki = dot(gs, q, 0, 0)
                vi = dot(sc_ref[h, ts, :cols], ga, 0, 0)
                q_ref[ts, lanes(h)] = gq.astype(BF16)
                for j in range(b + 1):
                    js = slice(j * tile, (j + 1) * tile)
                    kis[j] = ki[js] if kis[j] is None else kis[j] + ki[js]
                    vis[j] = vi[js] if vis[j] is None else vis[j] + vi[js]
            for j in range(tiles):
                ki_ref[i, j * tile : (j + 1) * tile, :] = kis[j]
                vi_ref[i, j * tile : (j + 1) * tile, :] = vis[j]

        each_head(g, one)

        @pl.when(g == 0)
        def _():
            relay_back(0)

        def finish(h, i):
            w = weight_of(h)
            later = brecv[h]
            k = k_ref[:, lanes(h)]
            k_ref[:, lanes(h)] = (ki_ref[i] + w * dot(v_ref[:, lanes(h)], later, 1, 1)).astype(BF16)
            g_ref[:, lanes(h)] = (vi_ref[i] + w * dot(k, later, 1, 0)).astype(BF16)

        each_head(g, finish)
        gk_copy(g).start()
        store(0, g).start()
        store(1, g).start()

        @pl.when(g == 0)
        def _():
            def rest(r, c):
                relay_back(r)
                return c

            lax.fori_loop(1, groups, rest, 0)

            def have_x(z, c):
                x_copy(z).wait_recv()
                return c

            lax.fori_loop(0, n, have_x, 0)

        gk_copy(g).wait_recv()
        scatter(g)
        return c

    lax.fori_loop(0, groups, grads_group, 0)

    def settle(g):
        @pl.when(me > 0)
        def _():
            arrived(me, g)
            out_ref[:, columns(g)] += st_ref[me, g].astype(F32)

        @pl.when(me < n - 1)
        def _():
            arrived(n, g)
            out_ref[:, columns(g)] += st_ref[n, g].astype(F32)

        store(2, g).start()

    each_group(settle)

    def drain(g):
        @pl.when(me < n - 1)
        def _():
            forward(g).wait_send()

        @pl.when(me > 0)
        def _():
            backward(g).wait_send()

        gk_copy(g).wait_send()
        for a in range(3):
            store(a, g).wait()

        def step(i, c):
            d, z, active = route(i)

            @pl.when(active)
            def _():
                term(d, z, g).wait_send()
            return c

        lax.fori_loop(0, (n - 1) * 2, step, 0)

    each_group(drain)

    def sent_x(z, c):
        x_copy(z).wait_send()
        return c

    lax.fori_loop(0, n, sent_x, 0)


def layer(lengths, log_decay, x, q, k, v, g):
    heads, B = log_decay.shape
    D, F = x.shape[1], q.shape[1]
    n = lax.axis_size("seq")
    rows = D // (2 * n)
    group = math.gcd(heads, 4)
    groups = heads // group
    hbm = pl.BlockSpec(memory_space=pl.ANY)
    state = (heads, LANES, LANES)
    wide = jax.ShapeDtypeStruct((B, F), BF16)
    dma = pltpu.SemaphoreType.DMA
    return pl.pallas_call(
        functools.partial(layer_kernel, heads),
        out_shape=(wide, wide, jax.ShapeDtypeStruct((rows, F), F32)),
        in_specs=[
            pl.BlockSpec(memory_space=pltpu.SMEM), pl.BlockSpec(memory_space=pltpu.VMEM)
        ] + [hbm] * 5,
        out_specs=(hbm, hbm, hbm),
        scratch_shapes=[pltpu.VMEM((B, F), BF16)] * 4
        + [
            pltpu.VMEM((B, D), BF16),
            pltpu.VMEM((D, B), BF16),
            pltpu.VMEM((n, rows, B), BF16),
            pltpu.VMEM((B, F), BF16),
            pltpu.VMEM((n + 1, groups, rows, group * LANES), BF16),
            pltpu.VMEM((rows, F), F32),
            pltpu.VMEM((heads, B), F32),
            pltpu.VMEM((heads, B, LANES), F32),
            pltpu.VMEM((B, B), F32),
            pltpu.VMEM((B, LANES), F32),
            pltpu.VMEM((B, LANES), F32),
            pltpu.VMEM(state, F32),
            pltpu.VMEM((heads, B, LANES), F32),
            pltpu.VMEM((heads, B, B), BF16),
            pltpu.VMEM((heads, B, LANES), BF16),
            pltpu.VMEM(state, F32),
            pltpu.VMEM((group, B, LANES), F32),
            pltpu.VMEM((group, B, LANES), F32),
        ]
        + [pltpu.VMEM(state, BF16)] * 4
        + [dma((groups,))] * 4
        + [
            dma((4, groups)), dma(()), dma((3, groups)), dma((n,)), dma((n,)),
            dma((groups,)), dma((groups,)), dma((n, groups)), dma((n + 1, groups)),
        ],
        compiler_params=pltpu.CompilerParams(
            collective_id=0, has_side_effects=True, vmem_limit_bytes=62 * 1024 * 1024
        ),
        name="layer",
    )(lengths, log_decay, x, q, k, v, g)


def body(inputs, queries, keys, values, log_decay, list_lengths, grad_out):
    gq, gv, gw = layer(
        list_lengths, log_decay[0], inputs[0], queries[0], keys[0], values[0], grad_out[0]
    )
    return gq[None], gv[None], gw


def solution(mesh):
    rows = ("groups", "dp")
    wide = P(rows, "seq", "head")
    return jax.shard_map(
        body,
        mesh=mesh,
        in_specs=(
            P(rows, "seq", None), wide, wide, wide, P(rows, "head", "seq"), P(rows, None), wide,
        ),
        out_specs=(wide, wide, P(("groups", "seq", "dp"), "head")),
        check_vma=False,
    )
```

time: 192 us -> 168 us (0.88)
  Pallas kernels: 179 us -> 158 us
  local copies, waits for them, and re-layouts: 11.7 us -> 7.62 us
    pallas_call x2 -> x1, Pallas kernels: 179 us -> 158 us  [layer(): pl.pallas_call(functools.partial(layer_kernel, heads), out_shape=(wide, w...]
    unnamed x10 -> x7, local copies, waits for them, and re-layouts: 9.84 us -> 7.62 us
where the time goes in v1:
time: 168 us; the launch traced here: 166 us
  Pallas kernels  158 us (94%)
  local copies, waits for them, and re-layouts  7.62 us (5%)
    pallas_call x1, Pallas kernels, layer(): pl.pallas_call(functools.partial(layer_kernel, heads), out_shape=(wide, w...  158 us
    unnamed x7, local copies, waits for them, and re-layouts  7.62 us

profile of v1, /device:TPU:9, one launch (start us, length us, event | category | flops | bytes accessed | tf_op | source)
XLA Modules:
  0.0 166.3 jit_solution(5973074722508222142)
XLA Ops:
  0.6 158.1 %layer.1 = (bf16[512,2048]{1,0:T(8,128)(2,1)}, bf16[512,2048]{1,0:T(8,128)(2,1)}, f32[384,2048]{1,0:T(8,128)}) custom-call(s32[1,4]{1,0:T(1,128)} %ll_ref.1, f32[16,512]{1,0:T(8,128)} %bitcast.15, bf16[512,3072]{1,0:T(8,128)(2,1)} %bitcast.8, bf16[512,2048]{1,0:T(8,128)(2,1)} %bitcast.11, bf16[512,2048]{1,0:T(8,128)(2,1)} %bitcast.12, ...), custom_call_target="tpu_custom_call" | custom-call | tf_op jit(solution)/shard_map/layer/pallas_call | solution.py:461
  158.7 0.0 copy-start.1
  158.7 3.3 %copy.13 = bf16[1,512,2048]{2,1,0:T(8,128)(2,1)} copy(bf16[1,512,2048]{2,1,0:T(8,128)(2,1)} %bitcast.10) | data formatting | bytes 4194304
  162.0 0.0 copy-done.1
  162.0 0.0 copy-start
  162.0 1.3 copy.14
  163.4 1.3 copy-done
  164.7 1.7 %copy.15 = f32[384,2048]{1,0:T(8,128)} copy(f32[384,2048]{1,0:T(8,128)S(1)} %copy-done) | data formatting | bytes 6291456
Async XLA Ops:
  158.7 3.3 %copy-start.1 = (bf16[512,2048]{1,0:T(8,128)(2,1)S(1)}, bf16[512,2048]{1,0:T(8,128)(2,1)}, u32[]{:S(2)}) copy-start(bf16[512,2048]{1,0:T(8,128)(2,1)} %get-tuple-element.7) | copy-start | bytes 6291460
  162.0 2.6 %copy-start = (f32[384,2048]{1,0:T(8,128)S(1)}, f32[384,2048]{1,0:T(8,128)}, u32[]{:S(2)}) copy-start(f32[384,2048]{1,0:T(8,128)} %get-tuple-element.14) | copy-start | bytes 9437188

commit v2 on v1

--- a/solution.py
+++ b/solution.py
@@ -214,18 +214,18 @@
 
     lax.fori_loop(0, n, send_x, 0)
 
-    def intra_group(g, c):
+    def attend_group(g, c):
         load(2, g).wait()
 
-        def one(h, i):
+        def intra(h, i):
             for b in range(tiles):
                 ts, cols = slice(b * tile, (b + 1) * tile), (b + 1) * tile
                 s = dot(q_ref[ts, lanes(h)], k_ref[:cols, lanes(h)], 1, 1)
                 s_bf = (s * decay_of(h, b)).astype(BF16)
                 sc_ref[h, ts, :cols] = s_bf
-                att_ref[h, ts, :] = dot(s_bf, v_ref[:cols, lanes(h)], 1, 0)
-
-        each_head(g, one)
+                att_ref[i, ts, :] = dot(s_bf, v_ref[:cols, lanes(h)], 1, 0)
+
+        each_head(g, intra)
 
         @pl.when(me > 0)
         def _():
@@ -237,17 +237,13 @@
                 fsend[h] = (passing_of(h) * frecv[h].astype(F32) + upd_ref[h]).astype(BF16)
             each_head(g, send)
             forward(g).start()
-        return c
-
-    lax.fori_loop(0, groups, intra_group, 0)
-
-    def attend_group(g, c):
+
         load(3, g).wait()
 
         def one(h, i):
             gamma = gamma_of(h)
             q = q_ref[:, lanes(h)]
-            att = gamma * dot(q, frecv[h], 1, 0) + att_ref[h]
+            att = gamma * dot(q, frecv[h], 1, 0) + att_ref[i]
             inv = lax.rsqrt(jnp.mean(att * att, axis=-1, keepdims=True) + EPS)
             normed = att * inv
             wide = g_ref[:, lanes(h)].astype(F32)
@@ -364,9 +360,7 @@
 
         each_head(g, one)
 
-        @pl.when(g == 0)
-        def _():
-            relay_back(0)
+        relay_back(g)
 
         def finish(h, i):
             w = weight_of(h)
@@ -380,14 +374,17 @@
         store(0, g).start()
         store(1, g).start()
 
+        @pl.when(at_end)
+        def _():
+            ready(g)
+            scatter(g)
+        return c
+
+    at_end = (me == 0) | (me == n - 1)
+
+    def ready(g):
         @pl.when(g == 0)
         def _():
-            def rest(r, c):
-                relay_back(r)
-                return c
-
-            lax.fori_loop(1, groups, rest, 0)
-
             def have_x(z, c):
                 x_copy(z).wait_recv()
                 return c
@@ -395,10 +392,15 @@
             lax.fori_loop(0, n, have_x, 0)
 
         gk_copy(g).wait_recv()
-        scatter(g)
-        return c
 
     lax.fori_loop(0, groups, grads_group, 0)
+
+    @pl.when(jnp.logical_not(at_end))
+    def _():
+        def inner_group(g):
+            ready(g)
+            scatter(g)
+        each_group(inner_group)
 
     def settle(g):
         @pl.when(me > 0)
@@ -479,7 +481,7 @@
             pltpu.VMEM((B, LANES), F32),
             pltpu.VMEM((B, LANES), F32),
             pltpu.VMEM(state, F32),
-            pltpu.VMEM((heads, B, LANES), F32),
+            pltpu.VMEM((group, B, LANES), F32),
             pltpu.VMEM((heads, B, B), BF16),
             pltpu.VMEM((heads, B, LANES), BF16),
             pltpu.VMEM(state, F32),

time: 168 us -> 163 us (0.970)
  Pallas kernels: 158 us -> 154 us
    pallas_call x1, Pallas kernels: 158 us -> 154 us  [layer(): pl.pallas_call(functools.partial(layer_kernel, heads), out_shape=(wide, w...]
where the time goes in v2:
time: 163 us
  Pallas kernels  154 us (94%)
  local copies, waits for them, and re-layouts  7.62 us (5%)
    pallas_call x1, Pallas kernels, layer(): pl.pallas_call(functools.partial(layer_kernel, heads), out_shape=(wide, w...  154 us
    unnamed x7, local copies, waits for them, and re-layouts  7.62 us

profile of v2, /device:TPU:9, one launch (start us, length us, event | category | flops | bytes accessed | tf_op | source)
XLA Modules:
  0.0 162.8 jit_solution(15314152039743359375)
XLA Ops:
  0.6 154.5 %layer.1 = (bf16[512,2048]{1,0:T(8,128)(2,1)}, bf16[512,2048]{1,0:T(8,128)(2,1)}, f32[384,2048]{1,0:T(8,128)}) custom-call(s32[1,4]{1,0:T(1,128)} %ll_ref.1, f32[16,512]{1,0:T(8,128)} %bitcast.15, bf16[512,3072]{1,0:T(8,128)(2,1)} %bitcast.8, bf16[512,2048]{1,0:T(8,128)(2,1)} %bitcast.11, bf16[512,2048]{1,0:T(8,128)(2,1)} %bitcast.12, ...), custom_call_target="tpu_custom_call" | custom-call | tf_op jit(solution)/shard_map/layer/pallas_call | solution.py:463
  155.1 0.0 copy-start.1
  155.1 3.3 %copy.13 = bf16[1,512,2048]{2,1,0:T(8,128)(2,1)} copy(bf16[1,512,2048]{2,1,0:T(8,128)(2,1)} %bitcast.10) | data formatting | bytes 4194304
  158.5 0.0 copy-done.1
  158.5 0.0 copy-start
  158.5 1.3 copy.14
  159.8 1.3 copy-done
  161.1 1.7 %copy.15 = f32[384,2048]{1,0:T(8,128)} copy(f32[384,2048]{1,0:T(8,128)S(1)} %copy-done) | data formatting | bytes 6291456
Async XLA Ops:
  155.1 3.3 %copy-start.1 = (bf16[512,2048]{1,0:T(8,128)(2,1)S(1)}, bf16[512,2048]{1,0:T(8,128)(2,1)}, u32[]{:S(2)}) copy-start(bf16[512,2048]{1,0:T(8,128)(2,1)} %get-tuple-element.7) | copy-start | bytes 6291460
  158.5 2.6 %copy-start = (f32[384,2048]{1,0:T(8,128)S(1)}, f32[384,2048]{1,0:T(8,128)}, u32[]{:S(2)}) copy-start(f32[384,2048]{1,0:T(8,128)} %get-tuple-element.14) | copy-start | bytes 9437188

commit v3 on v2

--- a/solution.py
+++ b/solution.py
@@ -50,7 +50,7 @@
     n = lax.axis_size("seq")
     me = lax.axis_index("seq")
     B = q_ref.shape[0]
-    group = math.gcd(heads, 4)
+    group = math.gcd(heads, 2)
     groups = heads // group
     tile = math.gcd(B, 256)
     tiles = B // tile
@@ -189,15 +189,6 @@
 
     lax.fori_loop(0, groups, update_group, 0)
 
-    load_x.wait()
-
-    def turn(i, c):
-        span = pl.ds(pl.multiple_of(i * LANES, LANES), LANES)
-        xt_ref[span, :] = jnp.transpose(x_ref[:, span])
-        return c
-
-    lax.fori_loop(0, D // LANES, turn, 0)
-
     def share(z, owner):
         return pl.ds(pl.multiple_of((z * 2 + owner) * rows, math.gcd(rows, LANES)), rows)
 
@@ -208,11 +199,23 @@
             device_id={"dp": mate}, device_id_type=MESH,
         )
 
-    def send_x(z, c):
-        x_copy(z).start()
-        return c
-
-    lax.fori_loop(0, n, send_x, 0)
+    def turn_inputs():
+        load_x.wait()
+
+        def turn(i, c):
+            span = pl.ds(pl.multiple_of(i * LANES, LANES), LANES)
+            xt_ref[span, :] = jnp.transpose(x_ref[:, span])
+            return c
+
+        lax.fori_loop(0, D // LANES, turn, 0)
+
+        def send_x(z, c):
+            x_copy(z).start()
+            return c
+
+        lax.fori_loop(0, n, send_x, 0)
+
+    pl.when(me == n - 1)(turn_inputs)
 
     def attend_group(g, c):
         load(2, g).wait()
@@ -265,6 +268,7 @@
         return c
 
     lax.fori_loop(0, groups, attend_group, 0)
+    pl.when(me < n - 1)(turn_inputs)
 
     def gk_copy(g):
         return pltpu.make_async_remote_copy(
@@ -454,7 +458,7 @@
     D, F = x.shape[1], q.shape[1]
     n = lax.axis_size("seq")
     rows = D // (2 * n)
-    group = math.gcd(heads, 4)
+    group = math.gcd(heads, 2)
     groups = heads // group
     hbm = pl.BlockSpec(memory_space=pl.ANY)
     state = (heads, LANES, LANES)

time: 163 us -> 161 us (0.988)
    pallas_call x1, Pallas kernels: 154 us -> 153 us  [layer(): pl.pallas_call(functools.partial(layer_kernel, heads), out_shape=(wide, w...]
where the time goes in v3:
time: 161 us
  Pallas kernels  153 us (95%)
  local copies, waits for them, and re-layouts  7.62 us (5%)
    pallas_call x1, Pallas kernels, layer(): pl.pallas_call(functools.partial(layer_kernel, heads), out_shape=(wide, w...  153 us
    unnamed x7, local copies, waits for them, and re-layouts  7.62 us

profile of v3, /device:TPU:9, one launch (start us, length us, event | category | flops | bytes accessed | tf_op | source)
XLA Modules:
  0.0 160.9 jit_solution(1269103768842435859)
XLA Ops:
  0.6 152.6 %layer.1 = (bf16[512,2048]{1,0:T(8,128)(2,1)}, bf16[512,2048]{1,0:T(8,128)(2,1)}, f32[384,2048]{1,0:T(8,128)}) custom-call(s32[1,4]{1,0:T(1,128)} %ll_ref.1, f32[16,512]{1,0:T(8,128)} %bitcast.15, bf16[512,3072]{1,0:T(8,128)(2,1)} %bitcast.8, bf16[512,2048]{1,0:T(8,128)(2,1)} %bitcast.11, bf16[512,2048]{1,0:T(8,128)(2,1)} %bitcast.12, ...), custom_call_target="tpu_custom_call" | custom-call | tf_op jit(solution)/shard_map/layer/pallas_call | solution.py:467
  153.2 0.0 copy-start.1
  153.2 3.3 %copy.13 = bf16[1,512,2048]{2,1,0:T(8,128)(2,1)} copy(bf16[1,512,2048]{2,1,0:T(8,128)(2,1)} %bitcast.10) | data formatting | bytes 4194304
  156.5 0.0 copy-done.1
  156.5 0.0 copy-start
  156.5 1.3 copy.14
  157.9 1.3 copy-done
  159.2 1.7 %copy.15 = f32[384,2048]{1,0:T(8,128)} copy(f32[384,2048]{1,0:T(8,128)S(1)} %copy-done) | data formatting | bytes 6291456
Async XLA Ops:
  153.2 3.3 %copy-start.1 = (bf16[512,2048]{1,0:T(8,128)(2,1)S(1)}, bf16[512,2048]{1,0:T(8,128)(2,1)}, u32[]{:S(2)}) copy-start(bf16[512,2048]{1,0:T(8,128)(2,1)} %get-tuple-element.7) | copy-start | bytes 6291460
  156.5 2.6 %copy-start = (f32[384,2048]{1,0:T(8,128)S(1)}, f32[384,2048]{1,0:T(8,128)}, u32[]{:S(2)}) copy-start(f32[384,2048]{1,0:T(8,128)} %get-tuple-element.14) | copy-start | bytes 9437188

commit v4 on v3

--- a/solution.py
+++ b/solution.py
@@ -505,10 +505,50 @@
     )(lengths, log_decay, x, q, k, v, g)
 
 
+def deliver_kernel(pieces, *refs):
+    count = (len(refs) - 2) // 3
+    srcs, dsts, bufs = refs[:count], refs[count : 2 * count], refs[2 * count : 3 * count]
+    in_sem, out_sem = refs[3 * count :]
+    spans = []
+    for a in range(count):
+        size = srcs[a].shape[0] // pieces
+        spans += [(a, p, pl.ds(p * size, size)) for p in range(pieces)]
+
+    def load(a, p, span):
+        return pltpu.make_async_copy(srcs[a].at[span], bufs[a].at[span], in_sem.at[a, p])
+
+    def store(a, p, span):
+        return pltpu.make_async_copy(bufs[a].at[span], dsts[a].at[span], out_sem.at[a, p])
+
+    for item in spans:
+        load(*item).start()
+    for item in spans:
+        load(*item).wait()
+        store(*item).start()
+    for item in spans:
+        store(*item).wait()
+
+
+def deliver(*arrays):
+    pieces = 4
+    hbm = pl.BlockSpec(memory_space=pl.ANY)
+    sems = pltpu.SemaphoreType.DMA((len(arrays), pieces))
+    return pl.pallas_call(
+        functools.partial(deliver_kernel, pieces),
+        out_shape=tuple(jax.ShapeDtypeStruct(a.shape, a.dtype) for a in arrays),
+        in_specs=[hbm] * len(arrays),
+        out_specs=(hbm,) * len(arrays),
+        scratch_shapes=[pltpu.VMEM(a.shape, a.dtype) for a in arrays] + [sems, sems],
+        compiler_params=pltpu.CompilerParams(vmem_limit_bytes=60 * 1024 * 1024),
+        name="deliver",
+    )(*arrays)
+
+
 def body(inputs, queries, keys, values, log_decay, list_lengths, grad_out):
     gq, gv, gw = layer(
         list_lengths, log_decay[0], inputs[0], queries[0], keys[0], values[0], grad_out[0]
     )
+    gq, gv, gw = deliver(gq, gv, gw)
     return gq[None], gv[None], gw
 
 

time: 161 us -> 159 us (0.988)
  local copies, waits for them, and re-layouts: 7.62 us -> 0 us
  Pallas kernels: 153 us -> 159 us
    unnamed x7 -> x0, local copies, waits for them, and re-layouts: 7.62 us -> none
    pallas_call x0 -> x1, Pallas kernels: none -> 5.98 us  [deliver(): pl.pallas_call(functools.partial(deliver_kernel, pieces), out_shape=tuple...]
where the time goes in v4:
time: 159 us
  Pallas kernels  159 us (100%)
    pallas_call x1, Pallas kernels, layer(): pl.pallas_call(functools.partial(layer_kernel, heads), out_shape=(wide, w...  153 us
    pallas_call x1, Pallas kernels, deliver(): pl.pallas_call(functools.partial(deliver_kernel, pieces), out_shape=tuple...  5.98 us

profile of v4, /device:TPU:9, one launch (start us, length us, event | category | flops | bytes accessed | tf_op | source)
XLA Modules:
  0.0 159.2 jit_solution(13754609633783795275)
XLA Ops:
  0.6 152.6 %layer.1 = (bf16[512,2048]{1,0:T(8,128)(2,1)}, bf16[512,2048]{1,0:T(8,128)(2,1)}, f32[384,2048]{1,0:T(8,128)}) custom-call(s32[1,4]{1,0:T(1,128)} %ll_ref.1, f32[16,512]{1,0:T(8,128)} %bitcast.13, bf16[512,3072]{1,0:T(8,128)(2,1)} %bitcast.8, bf16[512,2048]{1,0:T(8,128)(2,1)} %bitcast.9, bf16[512,2048]{1,0:T(8,128)(2,1)} %bitcast.10, ...), custom_call_target="tpu_custom_call" | custom-call | tf_op jit(solution)/shard_map/layer/pallas_call | solution.py:467
  153.2 6.0 %deliver.1 = (bf16[512,2048]{1,0:T(8,128)(2,1)}, bf16[512,2048]{1,0:T(8,128)(2,1)}, f32[384,2048]{1,0:T(8,128)}) custom-call(bf16[512,2048]{1,0:T(8,128)(2,1)} %get-tuple-element.9.refs_0_, bf16[512,2048]{1,0:T(8,128)(2,1)} %get-tuple-element.10.refs_1_, f32[384,2048]{1,0:T(8,128)} %get-tuple-element.11.refs_2_), custom_call_target="tpu_custom_call" | custom-call | tf_op jit(solution)/shard_map/deliver/pallas_call | solution.py:536
